TPU v7x, 32 devices: a whole 2x2x4 slice. The times are simulated.
32 devices in a mesh: row: 4 (over z), col: 8 (over y, x, core).
Axes of the slice: x: 2, y: 2, z: 4, core: 2. Of those that a mesh axis runs over, the one named last changes fastest.
Arguments:
- inverse_block: float32 [3072, 3072], P('row', 'col'), may hold values from -0.28867513 to 0.28867513, as said below
- grid_position: int32 [3072], replicated, may hold values from 0 to 3071, each once
- panel_a: float32 [512, 3072], P('row', 'col'), may hold values from -1.5 to 1.5
- pivot_inverse_a: float32 [512, 512], replicated, may hold values from -6 to 6
- chosen_rows: int32 [2048], replicated, may hold values from 0 to 3071, as said below
- top_panel_b: float32 [512, 512], replicated, may hold values from -1.5 to 1.5
- panel_b: float32 [512, 2048], P('row', 'col'), may hold values from -1.5 to 1.5
- pivot_inverse_b: float32 [512, 512], replicated, may hold values from -6 to 6
Outputs:
- inverse_panel_a: float32 [3072, 512], P(('row', 'col'))
- diagonal_a: float32 [512, 512], replicated
- inverse_panel_b: float32 [3072, 512], P(('row', 'col'))
- inverse_top_b: float32 [512, 512], replicated
- diagonal_b: float32 [512, 512], replicated
Inputs may be any that keep to these rules, and one draw needn't show every extreme that they name: `grid_position`: each of 0 to 3071 appears once. `chosen_rows`: 2048 distinct values. `inverse_block`: symmetric: entry (i, j) equals entry (j, i) in grid storage order.
All inputs are finite; a program needn't handle non-finite values.
Results may differ from a plain program's by a relative error of at most 0.00008.
Values sent between devices are 32-bit elements; how exact they have to be, the bound alone decides.
No kernel may reach another device: no remote copies, remote signals or barrier semaphores. Data moves between devices by JAX's collectives and lax.ppermute only.
A program may use at most 128 MiB of HBM per device.

v0:
```python
import jax
import jax.numpy as jnp
from jax import lax
from jax.sharding import PartitionSpec as P


def pick_columns(wide, index, limit):
    valid = (index < limit).astype(jnp.float32)
    taken = jnp.take(wide, jnp.minimum(index, limit - 1), axis=1)
    return taken * valid[None, :]


def select_columns(wide, source, start, length, limit):
    index = lax.dynamic_slice_in_dim(source, start, length, 0)
    return pick_columns(wide, index, limit)


def project(block, panel_t):
    return lax.dot_general(
        block,
        panel_t,
        (((1,), (1,)), ((), ())),
        precision=lax.Precision.HIGHEST,
        preferred_element_type=jnp.float32,
    )


def body(
    inverse_block,
    grid_position,
    panel_a,
    pivot_inverse_a,
    chosen_rows,
    top_panel_b,
    panel_b,
    pivot_inverse_b,
):
    exact = lax.Precision.HIGHEST
    rows_here = inverse_block.shape[0]
    cols_here = inverse_block.shape[1]
    order = grid_position.shape[0]
    count = chosen_rows.shape[0]
    width = top_panel_b.shape[0]
    row_count = lax.axis_size("row")
    own_rows = rows_here // lax.axis_size("col")
    col_start = lax.axis_index("col") * cols_here
    own_start = lax.axis_index("row") * rows_here + lax.axis_index("col") * own_rows
    group_starts = (
        jnp.arange(row_count, dtype=jnp.int32) * rows_here + lax.axis_index("col") * own_rows
    )
    group_index = (group_starts[:, None] + jnp.arange(own_rows, dtype=jnp.int32)[None, :]).reshape(
        -1
    )
    local_offset = lax.axis_index("row") * own_rows
    source_a = (
        jnp.zeros((order,), jnp.int32).at[grid_position].set(jnp.arange(order, dtype=jnp.int32))
    )
    source_b = (
        jnp.full((order,), count, jnp.int32)
        .at[grid_position[chosen_rows]]
        .set(jnp.arange(count, dtype=jnp.int32))
    )
    group_a = source_a[group_index]
    group_b = source_b[group_index]
    valid_own = (lax.dynamic_slice_in_dim(source_b, own_start, own_rows, 0) < count).astype(
        jnp.float32
    )
    wide_a, wide_b = (
        lax.all_gather(panel_a, "col", axis=1, tiled=True),
        lax.all_gather(panel_b, "col", axis=1, tiled=True),
    )
    cols_a, group_own_a, cols_b, group_own_b = (
        lax.all_gather(
            select_columns(wide_a, source_a, col_start, cols_here, order), "row", axis=0, tiled=True
        ),
        lax.all_gather(pick_columns(wide_a, group_a, order), "row", axis=0, tiled=True),
        lax.all_gather(
            select_columns(wide_b, source_b, col_start, cols_here, count), "row", axis=0, tiled=True
        ),
        lax.all_gather(pick_columns(wide_b, group_b, count), "row", axis=0, tiled=True),
    )
    stacked = jnp.concatenate([cols_a, cols_b], axis=0)
    product = lax.psum_scatter(
        project(inverse_block, stacked), "col", scatter_dimension=0, tiled=True
    )
    product_a = product[:, :width]
    product_b = product[:, width:]
    own_a = lax.dynamic_slice_in_dim(group_own_a, local_offset, own_rows, 1)
    own_b = lax.dynamic_slice_in_dim(group_own_b, local_offset, own_rows, 1)
    inverse_panel_a = -product_a
    diag_part = jnp.dot(own_a, inverse_panel_a, precision=exact, preferred_element_type=jnp.float32)
    cross_part = lax.dot_general(
        inverse_panel_a,
        own_b,
        (((0,), (1,)), ((), ())),
        precision=exact,
        preferred_element_type=jnp.float32,
    )
    diag_total, cross = lax.psum((diag_part, cross_part), ("row", "col"))
    diagonal_a = pivot_inverse_a - diag_total
    inverse_top_b = -(
        jnp.dot(diagonal_a, top_panel_b, precision=exact, preferred_element_type=jnp.float32)
        + cross
    )
    bottom = product_b + jnp.dot(
        inverse_panel_a, top_panel_b, precision=exact, preferred_element_type=jnp.float32
    )
    inverse_panel_b = -bottom * valid_own[:, None]
    last_part = jnp.dot(own_b, inverse_panel_b, precision=exact, preferred_element_type=jnp.float32)
    last_total = lax.psum(last_part, ("row", "col"))
    diagonal_b = (
        pivot_inverse_b
        - jnp.dot(top_panel_b.T, inverse_top_b, precision=exact, preferred_element_type=jnp.float32)
        - last_total
    )
    return (inverse_panel_a, diagonal_a, inverse_panel_b, inverse_top_b, diagonal_b)


def solution(mesh):
    in_specs = (P("row", "col"), P(), P("row", "col"), P(), P(), P(), P("row", "col"), P())
    out_specs = (P(("row", "col"), None), P(), P(("row", "col"), None), P(), P())
    return jax.shard_map(body, mesh=mesh, in_specs=in_specs, out_specs=out_specs, check_vma=False)
```

profile of v0, /device:TPU:0, one launch (start us, length us, event | category | flops | bytes accessed | tf_op | source)
XLA Modules:
  0.0 312.6 jit_solution(2024359006244433985)
XLA Ops:
  7.2 0.0 copy-start
  7.2 0.0 copy-start.1
  7.2 0.0 all-gather.5.cloned.1.call-start
  7.2 1.7 copy.30
  9.0 0.0 all-gather.5.cloned.1.call-update
  9.0 0.0 all-gather.3.cloned.1.call-start
  9.1 1.7 copy.29
  10.8 0.0 all-gather.3.cloned.1.call-update
  10.8 0.0 reduce-scatter.4.cloned.1.call-start
  10.9 0.7 fusion.14
  11.6 0.0 copy-done.1
  11.6 11.8 %gather_fusion = s32[2048]{0:T(1024)S(1)} fusion(s32[3072]{0:T(1024)S(1)} %copy-done.1, s32[2048]{0:T(1024)S(1)} %fusion.14), kind=kCustom, calls=%fused_computation.4 | custom fusion | bytes 24576 | tf_op jit(solution)/shard_map/gather | solution.py:60
  23.4 11.8 %scatter_custom_fusion = s32[3072]{0:T(1024)S(1)} fusion(s32[3072]{0:T(1024)S(1)} %compare_select_fusion.1, s32[3072]{0:T(1024)S(1)} %iota.15, s32[]{:T(128)} %constant.3.clone.1), kind=kCustom, calls=%fused_computation.38 | custom fusion | bytes 12292 | tf_op jit(solution)/shard_map/scatter | solution.py:56
  35.2 8.1 %scatter_custom_fusion.1 = s32[3072]{0:T(1024)S(1)} fusion(s32[2048]{0:T(1024)S(1)} %bitcast.29, s32[2048]{0:T(1024)S(1)} %iota.16, s32[]{:T(128)} %constant.8.clone.1), kind=kCustom, calls=%fused_computation.36 | custom fusion | bytes 12292 | tf_op jit(solution)/shard_map/scatter | solution.py:61
  43.3 0.1 compare_and_fusion.2
  43.4 0.1 compare_and_fusion.3
  43.5 0.0 all-gather.5.cloned.1.call-done
  43.5 2.3 gather_fusion.4
  45.9 0.2 bitcast_multiply_fusion.2
  46.0 21.3 %all_gather.21 = f32[512,384]{0,1:T(8,128)S(1)} all-gather(f32[128,384]{0,1:T(8,128)S(1)} %bitcast_multiply_fusion.2), channel_id=1, replica_groups=mesh['row'=4,'col'=8] {'row'}, dimensions={0}, use_global_device_ids=true | all-gather | bytes 983040 | tf_op jit(solution)/shard_map/all_gather | solution.py:77
  67.4 2.5 gather_fusion.3
  69.9 0.2 bitcast_multiply_fusion.3
  70.1 18.1 %all_gather.19 = f32[512,384]{0,1:T(8,128)S(1)} all-gather(f32[128,384]{0,1:T(8,128)S(1)} %bitcast_multiply_fusion.3), channel_id=1, replica_groups=mesh['row'=4,'col'=8] {'row'}, dimensions={0}, use_global_device_ids=true | all-gather | bytes 983040 | tf_op jit(solution)/shard_map/all_gather | solution.py:73
  88.2 9.6 %convolution_bitcast_fusion = f32[768,1024]{0,1:T(8,128)} fusion(f32[768,384]{1,0:T(8,128)S(1)} %copy-done, f32[512,384]{0,1:T(8,128)S(1)} %all_gather.21, f32[512,384]{0,1:T(8,128)S(1)} %all_gather.19), kind=kOutput, calls=%fused_computation.9 | convolution fusion | flops 3624271872 | bytes 5898240 | tf_op jit(solution)/shard_map/dot_general | solution.py:19
  97.8 3.5 %copy.37 = f32[768,1024]{1,0:T(8,128)} copy(f32[768,1024]{0,1:T(8,128)} %convolution_bitcast_fusion) | data formatting | bytes 6291456
  101.3 0.0 reduce-scatter.4.cloned.1.call-update
  101.3 0.0 all-reduce.3.cloned.1.call-start
  101.4 0.1 iota_add_fusion
  101.5 0.1 add.114
  101.6 2.5 gather_fusion.2
  104.1 0.0 copy-start.3
  104.2 2.5 gather_fusion.1
  106.7 0.1 compare_convert_fusion.1
  106.9 1.1 gather_fusion.6
  108.0 0.2 bitcast_multiply_fusion
  108.2 17.4 %all_gather.23 = f32[512,384]{0,1:T(8,128)S(1)} all-gather(f32[128,384]{0,1:T(8,128)S(1)} %bitcast_multiply_fusion), channel_id=1, replica_groups=mesh['row'=4,'col'=8] {'row'}, dimensions={0}, use_global_device_ids=true | all-gather | bytes 983040 | tf_op jit(solution)/shard_map/all_gather | solution.py:80
  125.6 2.5 gather_fusion.5
  128.1 0.2 bitcast_multiply_fusion.1
  128.3 17.9 %all_gather.22 = f32[512,384]{0,1:T(8,128)} all-gather(f32[128,384]{0,1:T(8,128)S(1)} %bitcast_multiply_fusion.1), channel_id=1, replica_groups=mesh['row'=4,'col'=8] {'row'}, dimensions={0}, use_global_device_ids=true | all-gather | bytes 983040 | tf_op jit(solution)/shard_map/all_gather | solution.py:76
  146.2 1.0 reduce-scatter.4.cloned.1.call-done
  147.2 0.9 slice.22
  148.1 0.1 copy.39
  148.2 0.0 copy-start.2
  148.2 3.0 fusion.8
  151.3 1.9 fusion.12
  153.2 0.7 fusion.7
  154.0 0.0 copy-start.8
  154.0 0.7 copy-done.8
  154.7 2.0 fusion.10
  156.7 0.0 all-reduce.3.cloned.1.call-update
  156.7 1.6 copy.32
  158.2 0.7 neg.9
  159.0 1.8 copy.34
  160.7 135.1 %all-reduce.3.cloned.1.call-done = (f32[512,512]{1,0:T(8,128)}, f32[512,512]{1,0:T(8,128)}, f32[512,512]{0,1:T(8,128)}) async-done(((f32[512,512]{1,0:T(8,128)}, f32[512,512]{1,0:T(8,128)}, f32[512,512]{0,1:T(8,128)}), (f32[512,512]{1,0:T(8,128)}, f32[512,512]{1,0:T(8,128)}, f32[512,512]{0,1:T(8,128)})) %all-reduce.3.cloned.1.call-update) | async-done | bytes 3145744 | tf_op jit(solution)/shard_map/psum | solution.py:99
  295.9 1.8 sub.9
  297.7 0.0 copy-start.4
  297.7 0.0 copy-done.7
  297.7 0.0 copy-start.6
  297.7 1.9 fusion.5
  299.6 0.0 copy-start.5
  299.6 1.0 copy-done.5
  300.6 0.0 copy-done.6
  300.6 3.0 fusion.4
  303.6 2.5 copy.35
  (23 shorter events, 0.1 us)
Async XLA Ops:
  7.2 81.0 %copy-start = (f32[768,384]{1,0:T(8,128)S(1)}, f32[768,384]{1,0:T(8,128)}, u32[]{:S(2)}) copy-start(f32[768,384]{1,0:T(8,128)} %param.12) | copy-start | bytes 3538948
  7.2 4.4 %copy-start.1 = (s32[3072]{0:T(1024)S(1)}, s32[3072]{0:T(1024)}, u32[]{:S(2)}) copy-start(s32[3072]{0:T(1024)} %param.13) | copy-start | bytes 36868
  7.2 36.3 %all-gather.5.cloned.1.call-start = ((), (), s32[]{:S(2)}) async-start(), calls=%async_computation.2 | async-start | bytes 1179648 | tf_op jit(solution)/shard_map/all_gather | solution.py:70
  9.0 58.4 %all-gather.3.cloned.1.call-start = ((), (), s32[]{:S(2)}) async-start(), calls=%async_computation.1 | async-start | bytes 1769472 | tf_op jit(solution)/shard_map/all_gather | solution.py:69
  10.8 136.3 %reduce-scatter.4.cloned.1.call-start = ((), (), s32[]{:S(2)}) async-start(), calls=%async_computation.3 | async-start | bytes 3538944 | tf_op jit(solution)/shard_map/reduce_scatter | solution.py:83
  101.3 194.5 %all-reduce.3.cloned.1.call-start = ((), (), s32[]{:S(2)}) async-start(), calls=%async_computation.4 | async-start | bytes 6291456 | tf_op jit(solution)/shard_map/psum | solution.py:99
  104.1 2.7 copy-start.3
  148.2 5.0 %copy-start.2 = (f32[512,512]{1,0:T(8,128)S(1)}, f32[512,512]{1,0:T(8,128)}, u32[]{:S(2)}) copy-start(f32[512,512]{1,0:T(8,128)} %param.17) | copy-start | bytes 3145732
  148.2 5.0 %copy-start.9 = (f32[96,1024]{1,0:T(8,128)S(1)}, f32[96,1024]{1,0:T(8,128)}, u32[]{:S(2)}) copy-start(f32[96,1024]{1,0:T(8,128)} %reduce-scatter.4.cloned.1.call-done) | copy-start | bytes 1179652
  154.0 0.7 copy-start.8
  295.8 1.9 copy-start.7
  297.7 1.9 copy-start.4
  297.7 2.9 copy-start.6
  299.6 1.0 copy-start.5
Sparse Core Ops, SparseCore 0:
  10.5 26.0 all-gather.4
  39.1 25.6 all-gather.2
  101.5 45.6 reduce-scatter.3
  156.8 138.9 all-reduce.2
where the time goes:
time: 313 us
  waiting for transfers between devices  136 us (43%)
  blocking collectives  74.8 us (24%)
  local copies, waits for them, and re-layouts  60.9 us (19%)
  matrix products  22.2 us (7%)
  between operations  14.1 us (5%)
  other arithmetic  4.37 us (1%)
    psum x1, waiting for transfers between devices, body(): diag_total, cross = lax.psum((diag_part, cross_part), ('row', 'col'))  135 us
    all_gather x1, blocking collectives, body(): lax.all_gather(select_columns(wide_b, source_b, col_start, cols_here, cou...  21.3 us
    all_gather x1, blocking collectives, body(): lax.all_gather(select_columns(wide_a, source_a, col_start, cols_here, ord...  18.1 us
    all_gather x1, blocking collectives, body(): lax.all_gather(pick_columns(wide_a, group_a, order), 'row', axis=0, tiled...  17.9 us
    all_gather x1, blocking collectives, body(): lax.all_gather(pick_columns(wide_b, group_b, count), 'row', axis=0, tiled...  17.4 us
    unnamed x27, local copies, waits for them, and re-layouts  14.6 us
    scatter x1, local copies, waits for them, and re-layouts, body(): jnp.zeros((order,), jnp.int32).at[grid_position]  11.8 us
    gather x1, local copies, waits for them, and re-layouts, body(): grid_position[chosen_rows]  11.8 us
  transfers between devices with their start and end apart: 4, of which 2 were waited for; matrix products, arithmetic and copies ran while one was open for 16% of the time, Pallas kernels for 0%

commit v1 on v0

--- a/solution.py
+++ b/solution.py
@@ -96,7 +96,7 @@
         precision=exact,
         preferred_element_type=jnp.float32,
     )
-    diag_total, cross = lax.psum((diag_part, cross_part), ("row", "col"))
+    diag_total, cross = lax.psum(lax.psum((diag_part, cross_part), "col"), "row")
     diagonal_a = pivot_inverse_a - diag_total
     inverse_top_b = -(
         jnp.dot(diagonal_a, top_panel_b, precision=exact, preferred_element_type=jnp.float32)

time: 313 us -> 451 us (1.44)
  waiting for transfers between devices: 136 us -> 272 us
    psum x1 -> x3, waiting for transfers between devices: 135 us -> 271 us  [the longest x1 130 us: body(): last_total = lax.psum(last_part, ('row', 'col'))]
    unnamed x27 -> x21, local copies, waits for them, and re-layouts: 14.6 us -> 14.6 us
  transfers between devices with their start and end apart: 4 -> 6, of which waited for: 2 -> 4; matrix products, arithmetic and copies ran while one was open for 16% -> 13% of each run, Pallas kernels for 0% -> 0%
where the time goes in v1:
time: 451 us
  waiting for transfers between devices  272 us (60%)
  blocking collectives  74.5 us (17%)
  local copies, waits for them, and re-layouts  60.9 us (14%)
  matrix products  24.6 us (5%)
  between operations  14.4 us (3%)
    psum x1, waiting for transfers between devices, body(): last_total = lax.psum(last_part, ('row', 'col'))  130 us
    psum x1, waiting for transfers between devices, body(): lax.psum(lax.psum((diag_part, cross_part), 'col'), 'row')  78.9 us
    psum x1, waiting for transfers between devices, body(): lax.psum((diag_part, cross_part), 'col')  61.9 us
    all_gather x1, blocking collectives, body(): lax.all_gather(select_columns(wide_b, source_b, col_start, cols_here, cou...  21.3 us
    all_gather x1, blocking collectives, body(): lax.all_gather(select_columns(wide_a, source_a, col_start, cols_here, ord...  18.1 us
    all_gather x1, blocking collectives, body(): lax.all_gather(pick_columns(wide_a, group_a, order), 'row', axis=0, tiled...  17.6 us
    all_gather x1, blocking collectives, body(): lax.all_gather(pick_columns(wide_b, group_b, count), 'row', axis=0, tiled...  17.4 us
    unnamed x21, local copies, waits for them, and re-layouts  14.6 us
  transfers between devices with their start and end apart: 6, of which 4 were waited for; matrix products, arithmetic and copies ran while one was open for 13% of the time, Pallas kernels for 0%

profile of v1, /device:TPU:0, one launch (start us, length us, event | category | flops | bytes accessed | tf_op | source)
XLA Modules:
  0.0 450.9 jit_solution(4935629794314745487)
XLA Ops:
  7.2 0.0 copy-start
  7.2 0.0 copy-start.1
  7.2 0.0 all-gather.5.cloned.1.call-start
  7.2 1.7 copy.30
  9.0 0.0 all-gather.5.cloned.1.call-update
  9.0 0.0 all-gather.3.cloned.1.call-start
  9.1 1.7 copy.29
  10.8 0.0 all-gather.3.cloned.1.call-update
  10.8 0.0 reduce-scatter.4.cloned.1.call-start
  10.9 0.7 fusion.14
  11.6 11.8 %gather_fusion = s32[2048]{0:T(1024)S(1)} fusion(s32[3072]{0:T(1024)S(1)} %copy-done.1, s32[2048]{0:T(1024)S(1)} %fusion.14), kind=kCustom, calls=%fused_computation.4 | custom fusion | bytes 24576 | tf_op jit(solution)/shard_map/gather | solution.py:60
  23.4 11.8 %scatter_custom_fusion = s32[3072]{0:T(1024)S(1)} fusion(s32[3072]{0:T(1024)S(1)} %compare_select_fusion.1, s32[3072]{0:T(1024)S(1)} %iota.15, s32[]{:T(128)} %constant.3.clone.1), kind=kCustom, calls=%fused_computation.38 | custom fusion | bytes 12292 | tf_op jit(solution)/shard_map/scatter | solution.py:56
  35.2 8.1 %scatter_custom_fusion.1 = s32[3072]{0:T(1024)S(1)} fusion(s32[2048]{0:T(1024)S(1)} %bitcast.29, s32[2048]{0:T(1024)S(1)} %iota.16, s32[]{:T(128)} %constant.8.clone.1), kind=kCustom, calls=%fused_computation.36 | custom fusion | bytes 12292 | tf_op jit(solution)/shard_map/scatter | solution.py:61
  43.3 0.1 compare_and_fusion.2
  43.4 0.1 compare_and_fusion.3
  43.5 0.0 all-gather.5.cloned.1.call-done
  43.5 2.3 gather_fusion.4
  45.9 0.2 bitcast_multiply_fusion.2
  46.0 21.3 %all_gather.21 = f32[512,384]{0,1:T(8,128)S(1)} all-gather(f32[128,384]{0,1:T(8,128)S(1)} %bitcast_multiply_fusion.2), channel_id=1, replica_groups=mesh['row'=4,'col'=8] {'row'}, dimensions={0}, use_global_device_ids=true | all-gather | bytes 983040 | tf_op jit(solution)/shard_map/all_gather | solution.py:77
  67.4 2.5 gather_fusion.3
  69.9 0.2 bitcast_multiply_fusion.3
  70.1 18.1 %all_gather.19 = f32[512,384]{0,1:T(8,128)S(1)} all-gather(f32[128,384]{0,1:T(8,128)S(1)} %bitcast_multiply_fusion.3), channel_id=1, replica_groups=mesh['row'=4,'col'=8] {'row'}, dimensions={0}, use_global_device_ids=true | all-gather | bytes 983040 | tf_op jit(solution)/shard_map/all_gather | solution.py:73
  88.2 9.6 %convolution_bitcast_fusion = f32[768,1024]{0,1:T(8,128)} fusion(f32[768,384]{1,0:T(8,128)S(1)} %copy-done, f32[512,384]{0,1:T(8,128)S(1)} %all_gather.21, f32[512,384]{0,1:T(8,128)S(1)} %all_gather.19), kind=kOutput, calls=%fused_computation.9 | convolution fusion | flops 3624271872 | bytes 5898240 | tf_op jit(solution)/shard_map/dot_general | solution.py:19
  97.8 3.5 copy.37
  101.3 0.0 reduce-scatter.4.cloned.1.call-update
  101.3 0.0 all-reduce.8.cloned.1.call-start
  101.4 0.1 iota_add_fusion
  101.5 0.1 add.118
  101.6 2.5 gather_fusion.2
  104.1 2.5 gather_fusion.1
  106.8 1.1 gather_fusion.6
  107.9 0.2 bitcast_multiply_fusion
  108.1 17.4 %all_gather.23 = f32[512,384]{0,1:T(8,128)S(1)} all-gather(f32[128,384]{0,1:T(8,128)S(1)} %bitcast_multiply_fusion), channel_id=1, replica_groups=mesh['row'=4,'col'=8] {'row'}, dimensions={0}, use_global_device_ids=true | all-gather | bytes 983040 | tf_op jit(solution)/shard_map/all_gather | solution.py:80
  125.5 2.5 gather_fusion.5
  128.0 0.2 bitcast_multiply_fusion.1
  128.2 17.6 %all_gather.22 = f32[512,384]{0,1:T(8,128)S(1)} all-gather(f32[128,384]{0,1:T(8,128)S(1)} %bitcast_multiply_fusion.1), channel_id=1, replica_groups=mesh['row'=4,'col'=8] {'row'}, dimensions={0}, use_global_device_ids=true | all-gather | bytes 983040 | tf_op jit(solution)/shard_map/all_gather | solution.py:76
  145.8 1.3 reduce-scatter.4.cloned.1.call-done
  147.1 0.9 slice.22
  148.1 0.1 copy.39
  148.2 2.0 fusion.8
  150.2 1.9 fusion.12
  152.2 0.0 all-reduce.8.cloned.1.call-update
  152.2 0.0 copy-start.2
  152.2 0.0 all-reduce.10.cloned.1.call-start
  152.2 61.9 %all-reduce.8.cloned.1.call-done = (f32[512,512]{1,0:T(8,128)}, f32[512,512]{1,0:T(8,128)}) async-done(((f32[512,512]{1,0:T(8,128)}, f32[512,512]{1,0:T(8,128)}), (f32[512,512]{1,0:T(8,128)}, f32[512,512]{1,0:T(8,128)})) %all-reduce.8.cloned.1.call-update) | async-done | bytes 2097168 | tf_op jit(solution)/shard_map/psum | solution.py:99
  214.2 0.0 all-reduce.10.cloned.1.call-update
  214.2 0.0 all-reduce.6.cloned.1.call-start
  214.2 0.1 compare_convert_fusion.1
  214.3 1.7 fusion.7
  216.0 0.0 copy-start.6
  216.0 0.7 copy-done.6
  216.7 2.0 fusion.10
  218.7 0.0 all-reduce.6.cloned.1.call-update
  218.7 1.6 copy.32
  220.3 0.7 neg.9
  221.0 1.8 copy.34
  222.7 78.9 %all-reduce.10.cloned.1.call-done = (f32[512,512]{1,0:T(8,128)}, f32[512,512]{1,0:T(8,128)}) async-done(((f32[512,512]{1,0:T(8,128)}, f32[512,512]{1,0:T(8,128)}), (f32[512,512]{1,0:T(8,128)}, f32[512,512]{1,0:T(8,128)})) %all-reduce.10.cloned.1.call-update) | async-done | bytes 2097168 | tf_op jit(solution)/shard_map/psum | solution.py:99
  301.7 1.8 sub.9
  303.5 0.0 copy-start.4
  303.5 1.0 copy-done.4
  304.5 2.9 fusion.5
  307.3 129.7 %all-reduce.6.cloned.1.call-done = f32[512,512]{0,1:T(8,128)} async-done(((f32[512,512]{0,1:T(8,128)}), f32[512,512]{0,1:T(8,128)}) %all-reduce.6.cloned.1.call-update) | async-done | bytes 1048592 | tf_op jit(solution)/shard_map/psum | solution.py:110
  437.0 4.5 fusion.4
  441.5 2.5 copy.35
  (23 shorter events, 0.1 us)
Async XLA Ops:
  7.2 81.0 %copy-start = (f32[768,384]{1,0:T(8,128)S(1)}, f32[768,384]{1,0:T(8,128)}, u32[]{:S(2)}) copy-start(f32[768,384]{1,0:T(8,128)} %param.12) | copy-start | bytes 3538948
  7.2 4.4 copy-start.1
  7.2 36.3 %all-gather.5.cloned.1.call-start = ((), (), s32[]{:S(2)}) async-start(), calls=%async_computation.2 | async-start | bytes 1179648 | tf_op jit(solution)/shard_map/all_gather | solution.py:70
  9.0 58.4 %all-gather.3.cloned.1.call-start = ((), (), s32[]{:S(2)}) async-start(), calls=%async_computation.1 | async-start | bytes 1769472 | tf_op jit(solution)/shard_map/all_gather | solution.py:69
  10.8 136.3 %reduce-scatter.4.cloned.1.call-start = ((), (), s32[]{:S(2)}) async-start(), calls=%async_computation.4 | async-start | bytes 3538944 | tf_op jit(solution)/shard_map/reduce_scatter | solution.py:83
  101.3 112.9 %all-reduce.8.cloned.1.call-start = ((), (), s32[]{:S(2)}) async-start(), calls=%async_computation.5 | async-start | bytes 4194304 | tf_op jit(solution)/shard_map/psum | solution.py:99
  104.1 2.6 copy-start.3
  152.2 62.1 %copy-start.2 = (f32[512,512]{1,0:T(8,128)S(1)}, f32[512,512]{1,0:T(8,128)}, u32[]{:S(2)}) copy-start(f32[512,512]{1,0:T(8,128)} %param.17) | copy-start | bytes 3145732
  152.2 149.5 %all-reduce.10.cloned.1.call-start = ((), (), s32[]{:S(2)}) async-start(), calls=%async_computation.6 | async-start | bytes 4194304 | tf_op jit(solution)/shard_map/psum | solution.py:99
  214.2 222.8 %all-reduce.6.cloned.1.call-start = ((), (), s32[]{:S(2)}) async-start(), calls=%async_computation.3 | async-start | bytes 2097152 | tf_op jit(solution)/shard_map/psum | solution.py:110
  216.0 0.7 copy-start.6
  301.7 2.8 copy-start.5
  303.5 1.0 copy-start.4
Sparse Core Ops, SparseCore 0:
  10.5 26.0 all-gather.4
  39.0 25.6 all-gather.2
  101.4 45.6 reduce-scatter.3
  152.3 61.8 all-reduce.7
  216.4 85.1 all-reduce.9
  307.3 129.7 all-reduce.5
